TPU v7x, 32 devices: a whole 2x2x4 slice. The times are simulated.
32 devices in a mesh: member: 2 (over x), row: 16 (over z, y, core).
Axes of the slice: x: 2, y: 2, z: 4, core: 2. Of those that a mesh axis runs over, the one named last changes fastest.
Arguments:
- innovation: bfloat16 [8, 1024, 2048], P('member', 'row'), parts along dimension 0, may hold values from -6 to 6
- background: bfloat16 [8, 1024, 2048], P('member', 'row'), parts along dimension 0, may hold values from -6 to 6
- level_weight: float32 [4], replicated, may hold values from 0.25 to 4
Outputs:
- displacement: float32 [4, 1024, 2048], P('member', 'row'), parts along dimension 0
There are 2 independent parts, one for each index of `member`. A program takes and returns all parts, laid end to end along the dimension named above; an argument that names none is the same for every part. Nothing has to cross between parts.
All inputs are finite; a program needn't handle non-finite values.
Results may differ from a plain program's by a relative error of at most 0.0003.
Values may be sent and summed in bfloat16 or wider, within the bound.
A program may use at most 64 MiB of HBM per device.

v0:
```python
import jax
import jax.numpy as jnp
from jax import lax
from jax.sharding import PartitionSpec as P

HALF = 64
SIGMA = 64


def padded_2(block, sides, width):
    for axis, dim in sides:
        count = lax.axis_size(axis)
        forward = [(i, i + 1) for i in range(count - 1)]
        backward = [(target, source) for source, target in forward]
        low = lax.ppermute(
            lax.slice_in_dim(block, block.shape[dim] - width, None, axis=dim), axis, forward
        )
        high = lax.ppermute(lax.slice_in_dim(block, 0, width, axis=dim), axis, backward)
        block = jnp.concatenate([low, block, high], axis=dim)
    return block


def tap_at(offset):
    grid = jnp.arange(-HALF, HALF + 1).astype(jnp.float32)
    spread = jnp.float32(SIGMA)
    total = jnp.sqrt(jnp.sum(jnp.exp(-grid * grid / (spread * spread))))
    off = offset.astype(jnp.float32)
    value = jnp.exp(-off * off / (2.0 * spread * spread)) / total
    return jnp.where(jnp.abs(offset) <= HALF, value, jnp.float32(0.0))


def band_blocks():
    inner = jnp.arange(128)[:, None]
    outer = jnp.arange(128)[None, :]
    return [tap_at(128 * shift + inner - outer) for shift in (-1, 0, 1)]


def smooth_last(values, blocks):
    lead = values.shape[:-1]
    length = values.shape[-1]
    nblocks = length // 128
    widths = [(0, 0)] * (values.ndim - 1) + [(128, 128)]
    padded = jnp.pad(values, widths).reshape(lead + (nblocks + 2, 128))
    total = jnp.zeros(lead + (nblocks, 128), jnp.float32)
    for index in range(3):
        part = padded[..., index : index + nblocks, :]
        total = total + jnp.dot(
            part, blocks[index], precision=lax.Precision.HIGHEST, preferred_element_type=jnp.float32
        )
    return total.reshape(lead + (length,))


def smooth_mid(values, blocks):
    chans, length, width = values.shape
    nblocks = length // 128
    padded = jnp.pad(values, ((0, 0), (128, 128), (0, 0))).reshape(chans, nblocks + 2, 128, width)
    total = jnp.zeros((chans, nblocks, 128, width), jnp.float32)
    for index in range(3):
        part = padded[:, index : index + nblocks]
        total = total + jnp.einsum(
            "cbix,io->cbox",
            part,
            blocks[index],
            precision=lax.Precision.HIGHEST,
            preferred_element_type=jnp.float32,
        )
    return total.reshape(chans, length, width)


def body(innovation, background, level_weight):
    blocks = band_blocks()
    rimmed = padded_2(background, (("row", 1),), 1).astype(jnp.float32)
    grad_y = 0.5 * (rimmed[:, 2:, :] - rimmed[:, :-2, :])
    padded_x = jnp.pad(rimmed[:, 1:-1, :], ((0, 0), (0, 0), (1, 1)))
    grad_x = 0.5 * (padded_x[:, :, 2:] - padded_x[:, :, :-2])
    scaled = level_weight[:, None, None] * innovation.astype(jnp.float32)
    numer_y = jnp.sum(scaled * grad_y, axis=0)
    numer_x = jnp.sum(scaled * grad_x, axis=0)
    denom = 1.0 + jnp.sum(level_weight[:, None, None] * (grad_y * grad_y + grad_x * grad_x), axis=0)
    raw = jnp.stack([numer_y / denom, numer_x / denom])
    zonal = smooth_last(raw, blocks)
    smoothed = smooth_mid(
        lax.all_to_all(zonal, "row", split_axis=2, concat_axis=1, tiled=True), blocks
    )
    return lax.all_to_all(smoothed, "row", split_axis=1, concat_axis=2, tiled=True)


def solution(mesh):
    placed = (P("member", "row", None), P("member", "row", None), P())
    return jax.shard_map(
        body, mesh=mesh, in_specs=placed, out_specs=P("member", "row", None), check_vma=False
    )
```

profile of v0, /device:TPU:1, one launch (start us, length us, event | category | flops | bytes accessed | tf_op | source)
XLA Modules:
  0.0 95.4 jit_solution(1240667817818672247)
XLA Ops:
  0.0 1.0 %fusion.82 = (bf16[4,1,2048]{2,1,0:T(2,128)(2,1)S(1)}, bf16[4,1,2048]{2,1,0:T(2,128)(2,1)S(1)}) fusion(bf16[4,64,2048]{2,1,0:T(8,128)(2,1)} %param.4), kind=kLoop, calls=%fused_computation.102 | loop fusion | bytes 65536 | tf_op jit(solution)/shard_map/slice | solution.py:16
  1.0 4.5 %collective-permute-start = (bf16[4,1,2048]{2,1,0:T(2,128)(2,1)S(1)}, bf16[4,1,2048]{2,1,0:T(2,128)(2,1)S(1)}, u32[]{:S(2)}, u32[]{:S(2)}) collective-permute-start(bf16[4,1,2048]{2,1,0:T(2,128)(2,1)S(1)} %get-tuple-element.8), channel_id=1, source_target_pairs={{0,1},{1,2},{2,3},{3,4},{4,5},{5,6},{6,7},{7,8},{8,9},{9,10},{10,1... | collective-permute-start | bytes 49160 | tf_op jit(solution)/shard_map/ppermute | solution.py:15
  5.6 1.9 %collective-permute-start.1 = (bf16[4,1,2048]{2,1,0:T(2,128)(2,1)S(1)}, bf16[4,1,2048]{2,1,0:T(2,128)(2,1)S(1)}, u32[]{:S(2)}, u32[]{:S(2)}) collective-permute-start(bf16[4,1,2048]{2,1,0:T(2,128)(2,1)S(1)} %get-tuple-element.9), channel_id=1, source_target_pairs={{1,0},{2,1},{3,2},{4,3},{5,4},{6,5},{7,6},{8,7},{9,8},{10,9},{11,1... | collective-permute-start | bytes 49160 | tf_op jit(solution)/shard_map/ppermute | solution.py:18
  7.5 0.6 fusion.63
  8.8 2.0 %collective-permute-done.1 = bf16[4,1,2048]{2,1,0:T(2,128)(2,1)S(1)} collective-permute-done((bf16[4,1,2048]{2,1,0:T(2,128)(2,1)S(1)}, bf16[4,1,2048]{2,1,0:T(2,128)(2,1)S(1)}, u32[]{:S(2)}, u32[]{:S(2)}) %collective-permute-start.1) | collective-permute-done | bytes 16416 | tf_op jit(solution)/shard_map/ppermute | solution.py:18
  10.8 1.6 %maximum_convert_fusion = f32[4,66,2048]{2,1,0:T(8,128)S(1)} fusion(bf16[4,1,2048]{2,1,0:T(2,128)(2,1)S(1)} %collective-permute-done.1, bf16[4,64,2048]{2,1,0:T(8,128)(2,1)} %param.4, bf16[4,1,2048]{2,1,0:T(2,128)(2,1)S(1)} %collective-permute-done), kind=kLoop, calls=%fused_computation.17 | loop fusion | flops 3244032 | bytes 3244032 | tf_op jit(solution)/shard_map/convert_element_type | solution.py:72
  12.4 0.0 copy-start
  12.4 0.0 copy-start.1
  12.4 0.3 slice.54
  12.7 0.9 copy-done
  13.6 2.7 %multiply_reduce_fusion.2 = (f32[64,2048]{1,0:T(8,128)S(1)}, f32[64,2048]{1,0:T(8,128)S(1)}, f32[64,2048]{1,0:T(8,128)S(1)}) fusion(bf16[4,64,2048]{2,1,0:T(8,128)(2,1)S(1)} %copy-done, f32[4]{0:T(128)S(1)} %copy-done.1, f32[4,66,2048]{2,1,0:T(8,128)S(1)} %maximum_convert_fusion, f32[4,64,2048]{2,1,0:T(8,128)S(1)} %slice.54), kind=kLoop, calls=%fused_computation.8 | loop fusion | flops 8519680 | bytes 8912912 | tf_op jit(solution)/shard_map/reduce_sum | solution.py:77
  16.3 0.1 divide_bitcast_fusion.1
  16.4 0.1 select_maximum_fusion
  16.5 0.2 reshape.52
  16.7 1.0 %fusion.10 = f32[2,64,16,128]{3,2,1,0:T(8,128)S(1)} fusion(f32[2,64,18,128]{3,2,1,0:T(8,128)S(1)} %reshape.52, f32[]{:T(128)S(6)} %sqrt.2, s32[128]{0:T(128)S(1)} %iota_add_fusion.1), kind=kOutput, calls=%fused_computation.25 | convolution fusion | flops 402800640 | bytes 2097668 | tf_op jit(solution)/shard_map/dot_general | solution.py:47
  17.7 1.0 %convolution_add_fusion.3 = f32[2,64,16,128]{3,2,1,0:T(8,128)S(1)} fusion(f32[2,64,16,128]{3,2,1,0:T(8,128)S(1)} %fusion.10, f32[2,64,18,128]{3,2,1,0:T(8,128)S(1)} %reshape.52, f32[]{:T(128)S(6)} %sqrt.2), kind=kOutput, calls=%fused_computation.15 | convolution fusion | flops 403062784 | bytes 3145732 | tf_op jit(solution)/shard_map/dot_general | solution.py:47
  18.7 1.0 %convolution_add_fusion.2 = f32[2,64,16,128]{3,2,1,0:T(8,128)S(1)} fusion(f32[2,64,16,128]{3,2,1,0:T(8,128)S(1)} %convolution_add_fusion.3, f32[2,64,18,128]{3,2,1,0:T(8,128)S(1)} %reshape.52, s32[128]{0:T(128)S(1)} %iota_add_fusion, f32[]{:T(128)S(6)} %sqrt.2), kind=kOutput, calls=%fused_computation.14 | convolution fusion | flops 403062784 | bytes 3146244 | tf_op jit(solution)/shard_map/dot_general | solution.py:47
  19.7 1.0 %copy.30 = f32[2,64,16,128]{1,0,3,2:T(2,128)S(1)} copy(f32[2,64,16,128]{3,2,1,0:T(8,128)S(1)} %convolution_add_fusion.2) | data formatting | bytes 2097152 | tf_op jit(solution)/shard_map/reshape | solution.py:50
  20.8 2.2 %reshape.62 = f32[16,1,16384]{2,1,0:T(1,128)S(1)} reshape(f32[2048,2,64]{2,1,0:T(2,128)S(1)} %bitcast.44) | data formatting | bytes 2097152
  23.0 30.9 %all_to_all.36 = f32[16,1,16384]{2,1,0:T(1,128)S(1)} all-to-all(f32[16,1,16384]{2,1,0:T(1,128)S(1)} %reshape.62), channel_id=1, replica_groups=mesh['member'=2,'row'=16] {'row'}, dimensions={0} | all-to-all | bytes 2097152 | tf_op jit(solution)/shard_map/all_to_all | solution.py:83
  53.8 0.5 broadcast.123
  54.3 3.1 %reduce = f32[16,16384]{1,0:T(8,128)S(1)} reduce(f32[16,1,16384]{2,1,0:T(1,128)S(1)} %all_to_all.36, f32[]{:T(128)} %broadcast.123), dimensions={1}, to_apply=%all_to_all.26.reduce_sub_computation | reduce | bytes 2097156 | tf_op jit(solution)/shard_map/all_to_all | solution.py:83
  57.5 1.5 %reshape.63 = f32[2048,2,64]{2,1,0:T(2,128)S(1)} reshape(f32[16,16384]{1,0:T(8,128)S(1)} %reduce) | data formatting | bytes 2097152
  59.0 0.9 copy.18
  60.0 0.1 pad.14
  60.1 1.1 %fusion.6 = f32[128,2,8,128]{3,0,2,1:T(8,128)S(1)} fusion(f32[2,10,128,128]{3,2,1,0:T(8,128)S(1)} %bitcast.41, f32[]{:T(128)S(6)} %sqrt.2, s32[128]{0:T(128)S(1)} %iota_add_fusion.1), kind=kOutput, calls=%fused_computation.21 | convolution fusion | flops 402800640 | bytes 2097668 | tf_op jit(solution)/shard_map/cbix,io->cbox/dot_general | solution.py:60
  61.1 1.1 %convolution_add_fusion.1 = f32[128,2,8,128]{3,0,2,1:T(8,128)S(1)} fusion(f32[128,2,8,128]{3,0,2,1:T(8,128)S(1)} %fusion.6, f32[2,10,128,128]{3,2,1,0:T(8,128)S(1)} %bitcast.42, f32[]{:T(128)S(6)} %sqrt.2), kind=kOutput, calls=%fused_computation.13 | convolution fusion | flops 403062784 | bytes 3145732 | tf_op jit(solution)/shard_map/cbix,io->cbox/dot_general | solution.py:60
  62.2 1.1 %convolution_add_fusion = f32[128,2,8,128]{3,0,2,1:T(8,128)S(1)} fusion(f32[128,2,8,128]{3,0,2,1:T(8,128)S(1)} %convolution_add_fusion.1, f32[2,10,128,128]{3,2,1,0:T(8,128)S(1)} %bitcast.43, s32[128]{0:T(128)S(1)} %iota_add_fusion, f32[]{:T(128)S(6)} %sqrt.2), kind=kOutput, calls=%fused_computation.12 | convolution fusion | flops 403062784 | bytes 3146244 | tf_op jit(solution)/shard_map/cbix,io->cbox/dot_general | solution.py:60
  63.3 0.8 copy.19
  64.1 29.5 %all_to_all.37 = f32[2,1024,128]{2,0,1:T(2,128)S(1)} all-to-all(f32[2,1024,128]{2,0,1:T(2,128)S(1)} %copy.19), channel_id=1, replica_groups=mesh['member'=2,'row'=16] {'row'}, dimensions={1} | all-to-all | bytes 2097152 | tf_op jit(solution)/shard_map/all_to_all | solution.py:85
  93.6 0.6 copy.20
  94.2 1.1 %all_to_all.33 = f32[2,64,2048]{2,1,0:T(8,128)} reshape(f32[2,64,16,128]{3,2,1,0:T(8,128)S(1)} %copy.20) | data formatting | bytes 2097152 | tf_op jit(solution)/shard_map/all_to_all | solution.py:85
  (4 shorter events, 0.0 us)
Async XLA Ops:
  1.0 7.8 %collective-permute-start = (bf16[4,1,2048]{2,1,0:T(2,128)(2,1)S(1)}, bf16[4,1,2048]{2,1,0:T(2,128)(2,1)S(1)}, u32[]{:S(2)}, u32[]{:S(2)}) collective-permute-start(bf16[4,1,2048]{2,1,0:T(2,128)(2,1)S(1)} %get-tuple-element.8), channel_id=1, source_target_pairs={{0,1},{1,2},{2,3},{3,4},{4,5},{5,6},{6,7},{7,8},{8,9},{9,10},{10,1... | collective-permute-start | bytes 49160 | tf_op jit(solution)/shard_map/ppermute | solution.py:15
  5.6 5.2 %collective-permute-start.1 = (bf16[4,1,2048]{2,1,0:T(2,128)(2,1)S(1)}, bf16[4,1,2048]{2,1,0:T(2,128)(2,1)S(1)}, u32[]{:S(2)}, u32[]{:S(2)}) collective-permute-start(bf16[4,1,2048]{2,1,0:T(2,128)(2,1)S(1)} %get-tuple-element.9), channel_id=1, source_target_pairs={{1,0},{2,1},{3,2},{4,3},{5,4},{6,5},{7,6},{8,7},{9,8},{10,9},{11,1... | collective-permute-start | bytes 49160 | tf_op jit(solution)/shard_map/ppermute | solution.py:18
  12.4 1.2 %copy-start = (bf16[4,64,2048]{2,1,0:T(8,128)(2,1)S(1)}, bf16[4,64,2048]{2,1,0:T(8,128)(2,1)}, u32[]{:S(2)}) copy-start(bf16[4,64,2048]{2,1,0:T(8,128)(2,1)} %param.3) | copy-start | bytes 3145732
  12.4 1.2 %copy-start.1 = (f32[4]{0:T(128)S(1)}, f32[4]{0:T(128)}, u32[]{:S(2)}) copy-start(f32[4]{0:T(128)} %param.5) | copy-start | bytes 52
where the time goes:
time: 95.7 us; the launch traced here: 95.4 us
  blocking collectives  60.4 us (63%)
  local copies, waits for them, and re-layouts  11.2 us (12%)
  other arithmetic  8.24 us (9%)
  starting transfers between devices  6.45 us (7%)
  matrix products  6.23 us (7%)
  waiting for transfers between devices  1.97 us (2%)
    all_to_all x1, blocking collectives, body(): lax.all_to_all(zonal, 'row', split_axis=2, concat_axis=1, tiled=True)  30.9 us
    all_to_all x1, blocking collectives, body(): lax.all_to_all(smoothed, 'row', split_axis=1, concat_axis=2, tiled=True)  29.5 us
    unnamed x6, local copies, waits for them, and re-layouts  4.65 us
    ppermute x1, starting transfers between devices, padded_2(): lax.ppermute(lax.slice_in_dim(block, block.shape[dim] - width, None, axis...  4.53 us
    dot_general x3, matrix products, smooth_mid(): jnp.einsum('cbix,io->cbox', part, blocks[index], precision=lax.Precision....  3.21 us
    all_to_all x1, other arithmetic, body(): lax.all_to_all(zonal, 'row', split_axis=2, concat_axis=1, tiled=True)  3.15 us
    dot_general x3, matrix products, smooth_last(): jnp.dot(part, blocks[index], precision=lax.Precision.HIGHEST, preferred_e...  3.02 us
    reduce_sum x1, other arithmetic, body(): numer_y = jnp.sum(scaled * grad_y, axis=0)  2.69 us
  transfers between devices with their start and end apart: 2, of which 1 were waited for; matrix products, arithmetic and copies ran while one was open for 1% of the time, Pallas kernels for 0%

commit v1 on v0

--- a/solution.py
+++ b/solution.py
@@ -5,6 +5,12 @@
 
 HALF = 64
 SIGMA = 64
+
+
+def swap_blocks(shard, axis, split, join):
+    parts = jnp.split(shard, lax.axis_size(axis), axis=split)
+    incoming = lax.all_to_all(jnp.stack(parts), axis, 0, 0)
+    return jnp.concatenate(incoming, axis=join)
 
 
 def padded_2(block, sides, width):
@@ -79,9 +85,7 @@
     denom = 1.0 + jnp.sum(level_weight[:, None, None] * (grad_y * grad_y + grad_x * grad_x), axis=0)
     raw = jnp.stack([numer_y / denom, numer_x / denom])
     zonal = smooth_last(raw, blocks)
-    smoothed = smooth_mid(
-        lax.all_to_all(zonal, "row", split_axis=2, concat_axis=1, tiled=True), blocks
-    )
+    smoothed = smooth_mid(swap_blocks(zonal, "row", 2, 1), blocks)
     return lax.all_to_all(smoothed, "row", split_axis=1, concat_axis=2, tiled=True)
 
 

time: 95.7 us -> 86.9 us (0.908)
  local copies, waits for them, and re-layouts: 11.2 us -> 5.44 us
  other arithmetic: 8.24 us -> 5.09 us
    unnamed x6 -> x19, local copies, waits for them, and re-layouts: 4.65 us -> 1.11 us
    all_to_all x1 -> x0, other arithmetic: 3.15 us -> none  [body(): lax.all_to_all(zonal, 'row', split_axis=2, concat_axis=1, tiled=True)]
    all_to_all x2 -> x1, local copies, waits for them, and re-layouts: 1.44 us -> 0.07 us  [swap_blocks(): incoming = lax.all_to_all(jnp.stack(parts), axis, 0, 0)]
where the time goes in v1:
time: 86.9 us; the launch traced here: 86.6 us
  blocking collectives  60.4 us (70%)
  starting transfers between devices  6.45 us (7%)
  matrix products  6.22 us (7%)
  local copies, waits for them, and re-layouts  5.44 us (6%)
  other arithmetic  5.09 us (6%)
  waiting for transfers between devices  1.97 us (2%)
  between operations  1 us (1%)
    all_to_all x1, blocking collectives, swap_blocks(): incoming = lax.all_to_all(jnp.stack(parts), axis, 0, 0)  30.9 us
    all_to_all x1, blocking collectives, body(): lax.all_to_all(smoothed, 'row', split_axis=1, concat_axis=2, tiled=True)  29.5 us
    ppermute x1, starting transfers between devices, padded_2(): lax.ppermute(lax.slice_in_dim(block, block.shape[dim] - width, None, axis...  4.53 us
    dot_general x3, matrix products, smooth_mid(): jnp.einsum('cbix,io->cbox', part, blocks[index], precision=lax.Precision....  3.21 us
    dot_general x3, matrix products, smooth_last(): jnp.dot(part, blocks[index], precision=lax.Precision.HIGHEST, preferred_e...  3.01 us
    reduce_sum x1, other arithmetic, body(): numer_y = jnp.sum(scaled * grad_y, axis=0)  2.69 us
    ppermute x1, waiting for transfers between devices, padded_2(): lax.ppermute(lax.slice_in_dim(block, 0, width, axis=dim), axis, backward)  1.96 us
    ppermute x1, starting transfers between devices, padded_2(): lax.ppermute(lax.slice_in_dim(block, 0, width, axis=dim), axis, backward)  1.92 us
  transfers between devices with their start and end apart: 2, of which 1 were waited for; matrix products, arithmetic and copies ran while one was open for 1% of the time, Pallas kernels for 0%

profile of v1, /device:TPU:1, one launch (start us, length us, event | category | flops | bytes accessed | tf_op | source)
XLA Modules:
  0.0 86.6 jit_solution(18088368372990632270)
XLA Ops:
  0.0 1.0 %fusion.98 = (bf16[4,1,2048]{2,1,0:T(2,128)(2,1)S(1)}, bf16[4,1,2048]{2,1,0:T(2,128)(2,1)S(1)}) fusion(bf16[4,64,2048]{2,1,0:T(8,128)(2,1)} %param.4), kind=kLoop, calls=%fused_computation.134 | loop fusion | bytes 65536 | tf_op jit(solution)/shard_map/slice | solution.py:22
  1.0 4.5 %collective-permute-start = (bf16[4,1,2048]{2,1,0:T(2,128)(2,1)S(1)}, bf16[4,1,2048]{2,1,0:T(2,128)(2,1)S(1)}, u32[]{:S(2)}, u32[]{:S(2)}) collective-permute-start(bf16[4,1,2048]{2,1,0:T(2,128)(2,1)S(1)} %get-tuple-element.8), channel_id=1, source_target_pairs={{0,1},{1,2},{2,3},{3,4},{4,5},{5,6},{6,7},{7,8},{8,9},{9,10},{10,1... | collective-permute-start | bytes 49160 | tf_op jit(solution)/shard_map/ppermute | solution.py:21
  5.6 1.9 %collective-permute-start.1 = (bf16[4,1,2048]{2,1,0:T(2,128)(2,1)S(1)}, bf16[4,1,2048]{2,1,0:T(2,128)(2,1)S(1)}, u32[]{:S(2)}, u32[]{:S(2)}) collective-permute-start(bf16[4,1,2048]{2,1,0:T(2,128)(2,1)S(1)} %get-tuple-element.9), channel_id=1, source_target_pairs={{1,0},{2,1},{3,2},{4,3},{5,4},{6,5},{7,6},{8,7},{9,8},{10,9},{11,1... | collective-permute-start | bytes 49160 | tf_op jit(solution)/shard_map/ppermute | solution.py:24
  7.5 0.6 fusion.79
  8.8 0.0 collective-permute-done
  8.8 2.0 %collective-permute-done.1 = bf16[4,1,2048]{2,1,0:T(2,128)(2,1)S(1)} collective-permute-done((bf16[4,1,2048]{2,1,0:T(2,128)(2,1)S(1)}, bf16[4,1,2048]{2,1,0:T(2,128)(2,1)S(1)}, u32[]{:S(2)}, u32[]{:S(2)}) %collective-permute-start.1) | collective-permute-done | bytes 16416 | tf_op jit(solution)/shard_map/ppermute | solution.py:24
  10.8 1.6 %maximum_convert_fusion = f32[4,66,2048]{2,1,0:T(8,128)S(1)} fusion(bf16[4,1,2048]{2,1,0:T(2,128)(2,1)S(1)} %collective-permute-done.1, bf16[4,64,2048]{2,1,0:T(8,128)(2,1)} %param.4, bf16[4,1,2048]{2,1,0:T(2,128)(2,1)S(1)} %collective-permute-done), kind=kLoop, calls=%fused_computation.17 | loop fusion | flops 3244032 | bytes 3244032 | tf_op jit(solution)/shard_map/convert_element_type | solution.py:78
  12.4 0.0 copy-start
  12.4 0.0 copy-start.1
  12.4 0.3 slice.54
  12.7 0.9 %copy-done = bf16[4,64,2048]{2,1,0:T(8,128)(2,1)S(1)} copy-done((bf16[4,64,2048]{2,1,0:T(8,128)(2,1)S(1)}, bf16[4,64,2048]{2,1,0:T(8,128)(2,1)}, u32[]{:S(2)}) %copy-start) | copy-done | bytes 1048600
  13.6 0.0 copy-done.1
  13.6 2.7 %multiply_reduce_fusion.2 = (f32[64,2048]{1,0:T(8,128)S(1)}, f32[64,2048]{1,0:T(8,128)S(1)}, f32[64,2048]{1,0:T(8,128)S(1)}) fusion(bf16[4,64,2048]{2,1,0:T(8,128)(2,1)S(1)} %copy-done, f32[4]{0:T(128)S(1)} %copy-done.1, f32[4,66,2048]{2,1,0:T(8,128)S(1)} %maximum_convert_fusion, f32[4,64,2048]{2,1,0:T(8,128)S(1)} %slice.54), kind=kLoop, calls=%fused_computation.8 | loop fusion | flops 8519680 | bytes 8912912 | tf_op jit(solution)/shard_map/reduce_sum | solution.py:83
  16.3 0.1 divide_bitcast_fusion.1
  16.4 0.1 select_maximum_fusion
  16.5 0.2 reshape.58
  16.7 1.0 %fusion.10 = f32[2,64,16,128]{3,2,1,0:T(8,128)S(1)} fusion(f32[2,64,18,128]{3,2,1,0:T(8,128)S(1)} %reshape.58, f32[]{:T(128)S(6)} %sqrt.2, s32[128]{0:T(128)S(1)} %iota_add_fusion.1), kind=kOutput, calls=%fused_computation.25 | convolution fusion | flops 402800640 | bytes 2097668 | tf_op jit(solution)/shard_map/dot_general | solution.py:53
  17.7 1.0 %convolution_add_fusion.3 = f32[2,64,16,128]{3,2,1,0:T(8,128)S(1)} fusion(f32[2,64,16,128]{3,2,1,0:T(8,128)S(1)} %fusion.10, f32[2,64,18,128]{3,2,1,0:T(8,128)S(1)} %reshape.58, f32[]{:T(128)S(6)} %sqrt.2), kind=kOutput, calls=%fused_computation.15 | convolution fusion | flops 403062784 | bytes 3145732 | tf_op jit(solution)/shard_map/dot_general | solution.py:53
  18.7 1.0 %convolution_add_fusion.2 = f32[2,64,16,128]{3,2,1,0:T(8,128)S(1)} fusion(f32[2,64,16,128]{3,2,1,0:T(8,128)S(1)} %convolution_add_fusion.3, f32[2,64,18,128]{3,2,1,0:T(8,128)S(1)} %reshape.58, s32[128]{0:T(128)S(1)} %iota_add_fusion, f32[]{:T(128)S(6)} %sqrt.2), kind=kOutput, calls=%fused_computation.14 | convolution fusion | flops 403062784 | bytes 3146244 | tf_op jit(solution)/shard_map/dot_general | solution.py:53
  19.7 0.2 reshape.59
  20.2 30.9 %all_to_all.23 = f32[16,2,64,128]{3,2,1,0:T(8,128)S(1)} all-to-all(f32[16,2,64,128]{3,2,1,0:T(8,128)S(1)} %fusion.27), channel_id=1, replica_groups=mesh['member'=2,'row'=16] {'row'}, dimensions={0} | all-to-all | bytes 2097152 | tf_op jit(solution)/shard_map/all_to_all | solution.py:12
  51.1 0.1 copy.30
  51.2 0.1 pad.14
  51.3 1.1 %fusion.6 = f32[128,2,8,128]{3,0,2,1:T(8,128)S(1)} fusion(f32[2,10,128,128]{3,2,1,0:T(8,128)S(1)} %bitcast.103, f32[]{:T(128)S(6)} %sqrt.2, s32[128]{0:T(128)S(1)} %iota_add_fusion.1), kind=kOutput, calls=%fused_computation.21 | convolution fusion | flops 402800640 | bytes 2097668 | tf_op jit(solution)/shard_map/cbix,io->cbox/dot_general | solution.py:66
  52.3 1.1 %convolution_add_fusion.1 = f32[128,2,8,128]{3,0,2,1:T(8,128)S(1)} fusion(f32[128,2,8,128]{3,0,2,1:T(8,128)S(1)} %fusion.6, f32[2,10,128,128]{3,2,1,0:T(8,128)S(1)} %bitcast.104, f32[]{:T(128)S(6)} %sqrt.2), kind=kOutput, calls=%fused_computation.13 | convolution fusion | flops 403062784 | bytes 3145732 | tf_op jit(solution)/shard_map/cbix,io->cbox/dot_general | solution.py:66
  53.4 1.1 %convolution_add_fusion = f32[128,2,8,128]{3,0,2,1:T(8,128)S(1)} fusion(f32[128,2,8,128]{3,0,2,1:T(8,128)S(1)} %convolution_add_fusion.1, f32[2,10,128,128]{3,2,1,0:T(8,128)S(1)} %bitcast.105, s32[128]{0:T(128)S(1)} %iota_add_fusion, f32[]{:T(128)S(6)} %sqrt.2), kind=kOutput, calls=%fused_computation.12 | convolution fusion | flops 403062784 | bytes 3146244 | tf_op jit(solution)/shard_map/cbix,io->cbox/dot_general | solution.py:66
  54.5 0.8 copy.31
  55.3 29.5 %all_to_all.24 = f32[2,1024,128]{2,0,1:T(2,128)S(1)} all-to-all(f32[2,1024,128]{2,0,1:T(2,128)S(1)} %copy.31), channel_id=1, replica_groups=mesh['member'=2,'row'=16] {'row'}, dimensions={1} | all-to-all | bytes 2097152 | tf_op jit(solution)/shard_map/all_to_all | solution.py:89
  84.8 0.6 copy.32
  85.4 1.1 %all_to_all.20 = f32[2,64,2048]{2,1,0:T(8,128)} reshape(f32[2,64,16,128]{3,2,1,0:T(8,128)S(1)} %copy.32) | data formatting | bytes 2097152 | tf_op jit(solution)/shard_map/all_to_all | solution.py:89
  (18 shorter events, 0.2 us)
Async XLA Ops:
  1.0 7.8 %collective-permute-start = (bf16[4,1,2048]{2,1,0:T(2,128)(2,1)S(1)}, bf16[4,1,2048]{2,1,0:T(2,128)(2,1)S(1)}, u32[]{:S(2)}, u32[]{:S(2)}) collective-permute-start(bf16[4,1,2048]{2,1,0:T(2,128)(2,1)S(1)} %get-tuple-element.8), channel_id=1, source_target_pairs={{0,1},{1,2},{2,3},{3,4},{4,5},{5,6},{6,7},{7,8},{8,9},{9,10},{10,1... | collective-permute-start | bytes 49160 | tf_op jit(solution)/shard_map/ppermute | solution.py:21
  5.6 5.2 %collective-permute-start.1 = (bf16[4,1,2048]{2,1,0:T(2,128)(2,1)S(1)}, bf16[4,1,2048]{2,1,0:T(2,128)(2,1)S(1)}, u32[]{:S(2)}, u32[]{:S(2)}) collective-permute-start(bf16[4,1,2048]{2,1,0:T(2,128)(2,1)S(1)} %get-tuple-element.9), channel_id=1, source_target_pairs={{1,0},{2,1},{3,2},{4,3},{5,4},{6,5},{7,6},{8,7},{9,8},{10,9},{11,1... | collective-permute-start | bytes 49160 | tf_op jit(solution)/shard_map/ppermute | solution.py:24
  12.4 1.2 %copy-start = (bf16[4,64,2048]{2,1,0:T(8,128)(2,1)S(1)}, bf16[4,64,2048]{2,1,0:T(8,128)(2,1)}, u32[]{:S(2)}) copy-start(bf16[4,64,2048]{2,1,0:T(8,128)(2,1)} %param.3) | copy-start | bytes 3145732
  12.4 1.2 %copy-start.1 = (f32[4]{0:T(128)S(1)}, f32[4]{0:T(128)}, u32[]{:S(2)}) copy-start(f32[4]{0:T(128)} %param.5) | copy-start | bytes 52
